TPU v7x, 256 devices: a whole 4x4x8 slice. The times are simulated.
256 devices in a mesh: gx: 32 (over y, x, core), gy: 8 (over z).
Axes of the slice: x: 4, y: 4, z: 8, core: 2. Of those that a mesh axis runs over, the one named last changes fastest.
Arguments:
- displacement: float32 [3, 32, 256, 1024], P(None, None, 'gx', 'gy'), may hold values from -6 to 6
- velocity: float32 [3, 32, 256, 1024], P(None, None, 'gx', 'gy'), may hold values from -6 to 6
- slopes: float32 [2, 32, 256, 1024], P(None, None, 'gx', 'gy'), may hold values from -0.5 to 0.5
- stretch: float32 [32, 256, 1024], P(None, 'gx', 'gy'), may hold values from 0.6 to 1.4
- moduli: float32 [2, 32, 256, 1024], P(None, None, 'gx', 'gy'), may hold values from 0.3 to 1
- buoyancy: float32 [32, 256, 1024], P(None, 'gx', 'gy'), may hold values from 0.5 to 1.5
- probes: float32 [4, 512, 128], P(None, 'gy'), may hold values from -0.0017089844 to 0.0017089844
Outputs:
- final_displacement: float32 [3, 32, 256, 1024], P(None, None, 'gx', 'gy')
- basis: float32 [128, 48, 128], P('gx', 'gy')
- factor: float32 [128, 128], replicated
All inputs are finite; a program needn't handle non-finite values.
Results may differ from a plain program's by a relative error of at most 0.0003.
Values sent between devices are 32-bit elements; how exact they have to be, the bound alone decides.
A program may use at most 64 MiB of HBM per device.

v0:
```python
import math
import jax
import jax.numpy as jnp
from jax import lax
from jax.sharding import PartitionSpec as P

STEPS = 4
time_step = 0.12


def extended(block, sides, width):
    for axis, dim in sides:
        count = lax.axis_size(axis)
        forward = [(i, i + 1) for i in range(count - 1)]
        backward = [(target, source) for source, target in forward]
        low = lax.ppermute(
            lax.slice_in_dim(block, block.shape[dim] - width, None, axis=dim), axis, forward
        )
        high = lax.ppermute(lax.slice_in_dim(block, 0, width, axis=dim), axis, backward)
        block = jnp.concatenate([low, block, high], axis=dim)
    return block


def fourth(values, dimension):
    length_out = values.shape[dimension] - 4

    def segment(offset):
        return lax.slice_in_dim(values, offset, offset + length_out, axis=dimension)

    return (segment(0) - segment(4) + 8.0 * (segment(3) - segment(1))) / 12.0


def vertical(values):
    padded = jnp.pad(values, ((0, 0), (2, 2), (0, 0), (0, 0)))
    return fourth(padded, 1)


def gradient(padded, slope_x, slope_y, stretch):
    d_x = fourth(padded[:, :, :, 2:-2], 2)
    d_y = fourth(padded[:, :, 2:-2, :], 3)
    d_r = vertical(padded[:, :, 2:-2, 2:-2])
    return jnp.stack([d_x + slope_x * d_r, d_y + slope_y * d_r, stretch * d_r], axis=1)


def stresses(gradients, lame, shear):
    divergence = gradients[0, 0] + gradients[1, 1] + gradients[2, 2]
    pressure = lame * divergence
    return jnp.stack(
        [
            pressure + 2.0 * shear * gradients[0, 0],
            pressure + 2.0 * shear * gradients[1, 1],
            pressure + 2.0 * shear * gradients[2, 2],
            shear * (gradients[0, 1] + gradients[1, 0]),
            shear * (gradients[0, 2] + gradients[2, 0]),
            shear * (gradients[1, 2] + gradients[2, 1]),
        ]
    )


def forces(padded, slope_x, slope_y, stretch):
    d_x = fourth(padded[:, :, :, 2:-2], 2)
    d_y = fourth(padded[:, :, 2:-2, :], 3)
    d_r = vertical(padded[:, :, 2:-2, 2:-2])
    rows_x = (0, 3, 4)
    rows_y = (3, 1, 5)
    rows_z = (4, 5, 2)
    return jnp.stack(
        [
            d_x[rows_x[component]]
            + slope_x * d_r[rows_x[component]]
            + d_y[rows_y[component]]
            + slope_y * d_r[rows_y[component]]
            + stretch * d_r[rows_z[component]]
            for component in range(3)
        ]
    )


def lower_factor(gram):
    order = gram.shape[0]
    positions = jnp.arange(order, dtype=jnp.int32)

    def column_step(column_index, lower):
        picker = (positions == column_index).astype(jnp.float32)
        column = jnp.dot(gram, picker, precision=lax.Precision.HIGHEST)
        row_of = jnp.dot(picker, lower, precision=lax.Precision.HIGHEST)
        column = column - jnp.dot(lower, row_of, precision=lax.Precision.HIGHEST)
        pivot = jnp.sqrt(jnp.sum(column * picker))
        entries = jnp.where(
            positions > column_index,
            column / pivot,
            jnp.where(positions == column_index, pivot, 0.0),
        )
        return lower + entries[:, None] * picker[None, :]

    return lax.fori_loop(0, order, column_step, jnp.zeros_like(gram))


def lower_inverse(lower):
    order = lower.shape[0]
    positions = jnp.arange(order, dtype=jnp.int32)

    def row_step(row_index, inverse):
        picker = (positions == row_index).astype(jnp.float32)
        row_of = jnp.dot(picker, lower, precision=lax.Precision.HIGHEST)
        pivot = jnp.sum(row_of * picker)
        fresh = (picker - jnp.dot(row_of, inverse, precision=lax.Precision.HIGHEST)) / pivot
        return inverse + picker[:, None] * fresh[None, :]

    return lax.fori_loop(0, order, row_step, jnp.zeros_like(lower))


def orthogonalize(tall_block, gram):
    lower = lower_factor(gram)
    inverse = lower_inverse(lower)
    result = jnp.dot(
        tall_block, inverse.T, precision=lax.Precision.HIGHEST, preferred_element_type=jnp.float32
    )
    return (result, lower.T)


def shards(displacement, velocity, slopes, stretch, moduli, buoyancy, probes):
    previous = displacement - time_step * velocity
    current = displacement
    for moment in range(STEPS):
        padded = extended(current, (("gx", 2), ("gy", 3)), 2)
        gradients = gradient(padded, slopes[0], slopes[1], stretch)
        stress = extended(stresses(gradients, moduli[0], moduli[1]), (("gx", 2), ("gy", 3)), 2)
        pushes = buoyancy * forces(stress, slopes[0], slopes[1], stretch)
        following = 2.0 * current - previous + time_step**2 * pushes
        velocities = (following - previous) / (2.0 * time_step)
        sampled = velocities[:, ::2, ::2, ::2]
        half_x = sampled.shape[2]
        rearranged = jnp.transpose(sampled, (2, 0, 1, 3)).reshape(-1, sampled.shape[3])
        sketch_term = jnp.dot(
            rearranged,
            probes[moment],
            precision=lax.Precision.HIGHEST,
            preferred_element_type=jnp.float32,
        ).reshape(half_x, -1, probes.shape[2])
        reduced = lax.psum_scatter(sketch_term, "gy", scatter_dimension=1, tiled=True)
        sketch = reduced if moment == 0 else sketch + reduced
        previous, current = (current, following)
    tall_block = sketch.reshape(-1, sketch.shape[2])
    rows_total = tall_block.shape[0] * lax.axis_size("gx") * lax.axis_size("gy")
    gram_local = jnp.dot(
        tall_block.T,
        tall_block,
        precision=lax.Precision.HIGHEST,
        preferred_element_type=jnp.float32,
    )
    gram_whole = lax.psum(gram_local, ("gx", "gy"))
    orthonormal, factor = orthogonalize(tall_block, gram_whole)
    basis = (math.sqrt(rows_total) * orthonormal).reshape(sketch.shape)
    return (current, basis, factor)


def solution(mesh):
    in_specs = (
        P(None, None, "gx", "gy"),
        P(None, None, "gx", "gy"),
        P(None, None, "gx", "gy"),
        P(None, "gx", "gy"),
        P(None, None, "gx", "gy"),
        P(None, "gx", "gy"),
        P(None, "gy", None),
    )
    out_specs = (P(None, None, "gx", "gy"), P("gx", "gy", None), P())
    return jax.shard_map(shards, mesh=mesh, in_specs=in_specs, out_specs=out_specs, check_vma=False)
```

profile of v0, /device:TPU:1, one launch (start us, length us, event | category | flops | bytes accessed | tf_op | source)
XLA Modules:
  0.0 1194.3 jit_solution(5939340690643367252)
XLA Ops:
  8.8 4.6 collective-permute-start
  13.4 2.0 collective-permute-start.1
  18.1 4.4 collective-permute-done.1
  26.6 4.9 collective-permute-start.2
  35.1 3.8 fusion.119
  42.7 1.8 fusion.162
  44.9 2.1 collective-permute-start.4
  47.0 2.2 collective-permute-start.5
  49.6 4.4 collective-permute-done.5
  56.2 2.4 copy.319
  59.1 3.6 collective-permute-start.6
  64.0 2.7 fusion.51
  69.5 2.4 copy.318
  71.9 3.0 fusion.94
  76.9 3.5 collective-permute-start.8
  80.4 1.9 collective-permute-start.9
  82.4 4.0 collective-permute-done.9
  89.0 3.7 collective-permute-start.10
  95.2 2.7 collective-permute-done.11
  99.3 2.1 fusion.155
  101.8 3.0 collective-permute-start.12
  104.8 1.9 collective-permute-start.13
  107.4 4.4 collective-permute-done.13
  111.8 1.8 fusion.291
  115.4 1.8 copy.329
  117.2 5.1 collective-permute-start.14
  125.4 2.5 collective-permute-done.15
  128.0 2.4 copy.332
  131.9 3.4 fusion.88
  136.6 2.9 collective-permute-start.16
  139.5 1.9 collective-permute-start.17
  141.4 6.0 slice.1072
  150.9 3.6 collective-permute-start.18
  157.0 2.4 collective-permute-done.19
  160.8 2.1 fusion.148
  163.3 5.1 collective-permute-start.20
  168.4 1.9 collective-permute-start.21
  171.9 6.0 slice.1074
  181.5 2.5 copy.342
  185.3 3.9 collective-permute-start.22
  190.5 2.7 fusion.41
  196.3 2.4 copy.341
  198.7 3.0 fusion.82
  202.2 5.1 collective-permute-start.24
  207.3 1.9 collective-permute-start.25
  210.9 2.5 slice.1076
  214.9 2.5 collective-permute-start.26
  220.1 2.0 collective-permute-done.27
  222.8 1.8 fusion.141
  225.0 5.1 collective-permute-start.28
  230.1 1.9 collective-permute-start.29
  233.0 4.0 collective-permute-done.29
  237.2 1.8 fusion.289
  239.0 2.4 copy.353
  243.1 3.7 collective-permute-start.30
  249.5 2.8 collective-permute-done.31
  252.3 2.4 copy.354
  254.7 2.4 copy.352
  257.1 3.4 fusion.76
  261.0 2.5 slice.1078
  266.5 78.0 %all-reduce.14.cloned.1.call-done = f32[4,48,128]{2,0,1:T(4,128)} async-done(((f32[4,48,128]{2,0,1:T(4,128)}), f32[4,48,128]{2,0,1:T(4,128)}) %all-reduce.14.cloned.1.call-update) | async-done | bytes 98320
  347.2 245.3 %all-reduce.12.cloned.1.call-done = f32[128,128]{1,0:T(8,128)} async-done(((f32[128,128]{1,0:T(8,128)}), f32[128,128]{1,0:T(8,128)}) %all-reduce.12.cloned.1.call-update) | async-done | bytes 65552 | tf_op jit(solution)/shard_map/psum | solution.py:152
  592.5 363.3 %while.30 = (s32[]{:T(128)}, f32[128,128]{1,0:T(8,128)S(1)}, f32[128,128]{1,0:T(8,128)}, s32[]{:T(128)}, s32[]{:T(128)}) while((s32[]{:T(128)}, f32[128,128]{1,0:T(8,128)S(1)}, f32[128,128]{1,0:T(8,128)}, s32[]{:T(128)}, s32[]{:T(128)}) %tuple.125), condition=%wide.region_7.8_spmd.clone.clone, body=%wide.region_5.7_spmd.clone.clone.sunk | while | flops 673410 | bytes 332917 | solution.py:96
  956.5 230.0 %while.29 = (s32[]{:T(128)}, f32[128,128]{1,0:T(8,128)S(1)}, f32[128,128]{1,0:T(8,128)S(1)}, s32[]{:T(128)}, s32[]{:T(128)}) while((s32[]{:T(128)}, f32[128,128]{1,0:T(8,128)S(1)}, f32[128,128]{1,0:T(8,128)S(1)}, s32[]{:T(128)}, s32[]{:T(128)}) %tuple.128), condition=%wide.region_10.11_spmd.clone, body=%wide.region_8.10_spmd.clone.sunk | while | flops 460034 | bytes 265316 | solution.py:110
  (1509 shorter events, 573.1 us)
Async XLA Ops:
  7.2 337.4 %all-reduce.14.cloned.1.call-start = ((), (), s32[]{:S(2)}) async-start(), calls=%async_computation.1 | async-start | bytes 196608
  8.7 6.7 copy-start.38
  8.7 6.7 copy-start.39
  8.7 6.8 copy-start.3
  8.8 7.5 copy-start.2
  8.8 9.3 collective-permute-start
  13.4 9.1 collective-permute-start.1
  15.5 29.0 %copy-start.4 = (f32[1,32,8,128]{3,2,1,0:T(8,128)}, f32[1,32,8,128]{3,2,1,0:T(8,128)S(1)}, u32[]{:S(2)}) copy-start(f32[1,32,8,128]{3,2,1,0:T(8,128)S(1)} %get-tuple-element.324) | copy-start | bytes 393220
  18.1 4.7 copy-start.23
  25.3 16.2 %collective-permute-start.3 = (f32[3,32,12,2]{1,3,2,0:T(2,128)}, f32[3,32,12,2]{1,3,2,0:T(2,128)}, u32[]{:S(2)}, u32[]{:S(2)}) collective-permute-start(f32[3,32,12,2]{1,3,2,0:T(2,128)} %get-tuple-element.276), channel_id=1, source_target_pairs={{1,0},{2,1},{3,2},{4,3},{5,4},{6,5},{7,6},{9,8},{10,9},{11,10},{12... | collective-permute-start | bytes 27656 | tf_op jit(solution)/shard_map/ppermute | solution.py:19
  26.6 12.3 %copy-start.1 = (f32[3,32,12,128]{1,3,2,0:T(8,128)S(1)}, f32[3,32,12,128]{1,3,2,0:T(8,128)}, u32[]{:S(2)}) copy-start(f32[3,32,12,128]{1,3,2,0:T(8,128)} %copy-done) | copy-start | bytes 1769476
  26.6 13.8 %collective-permute-start.2 = (f32[3,32,12,2]{1,3,2,0:T(2,128)}, f32[3,32,12,2]{1,3,2,0:T(2,128)}, u32[]{:S(2)}, u32[]{:S(2)}) collective-permute-start(f32[3,32,12,2]{1,3,2,0:T(2,128)} %get-tuple-element.277), channel_id=1, source_target_pairs={{0,1},{1,2},{2,3},{3,4},{4,5},{5,6},{6,7},{8,9},{9,10},{10,11},{11... | collective-permute-start | bytes 27656 | tf_op jit(solution)/shard_map/ppermute | solution.py:16
  40.4 2.2 copy-start.7
  40.4 2.2 copy-start.9
  40.4 2.2 copy-start.14
  44.7 4.5 copy-start.40
  44.9 4.7 collective-permute-start.4
  47.0 7.0 collective-permute-start.5
  49.6 4.4 copy-start.17
  59.1 10.4 collective-permute-start.6
  62.7 5.4 collective-permute-start.7
  71.9 3.0 copy-start.11
  71.9 3.0 copy-start.20
  76.9 5.5 collective-permute-start.8
  80.4 5.9 collective-permute-start.9
  86.4 7.7 copy-start.30
  89.0 9.1 collective-permute-start.10
  92.8 5.1 collective-permute-start.11
  95.2 4.1 copy-start.31
  101.8 5.6 collective-permute-start.12
  104.8 7.0 collective-permute-start.13
  117.2 13.2 %collective-permute-start.14 = (f32[6,32,12,2]{1,3,2,0:T(2,128)S(1)}, f32[6,32,12,2]{1,3,2,0:T(2,128)S(1)}, u32[]{:S(2)}, u32[]{:S(2)}) collective-permute-start(f32[6,32,12,2]{1,3,2,0:T(2,128)S(1)} %copy.329), channel_id=1, source_target_pairs={{0,1},{1,2},{2,3},{3,4},{4,5},{5,6},{6,7},{8,9},{9,10},{10,11},{11... | collective-permute-start | bytes 55304 | tf_op jit(solution)/shard_map/ppermute | solution.py:16
  122.3 5.7 collective-permute-start.15
  131.9 3.5 copy-start.12
  131.9 3.5 copy-start.21
  136.6 11.5 collective-permute-start.16
  139.5 8.6 collective-permute-start.17
  150.9 8.8 collective-permute-start.18
  154.5 4.8 collective-permute-start.19
  163.1 7.2 copy-start.33
  163.3 15.3 %collective-permute-start.20 = (f32[6,32,2,128]{3,1,2,0:T(8,128)S(1)}, f32[6,32,2,128]{3,1,2,0:T(8,128)S(1)}, u32[]{:S(2)}, u32[]{:S(2)}) collective-permute-start(f32[6,32,2,128]{3,1,2,0:T(8,128)S(1)} %get-tuple-element.294), channel_id=1, source_target_pairs={{0,8},{8,16},{16,24},{24,32},{32,40},{40,48},{48,56},{56,64},{64,7... | collective-permute-start | bytes 589832 | tf_op jit(solution)/shard_map/ppermute | solution.py:16
  168.4 10.2 collective-permute-start.21
  185.3 11.0 collective-permute-start.22
  189.3 5.7 collective-permute-start.23
  198.7 3.0 copy-start.13
  198.7 3.0 copy-start.22
  202.0 7.2 copy-start.34
  202.0 7.2 copy-start.36
  202.2 11.8 collective-permute-start.24
  207.3 6.7 collective-permute-start.25
  214.0 4.9 copy-start.29
  214.9 7.8 copy-start.8
  214.9 7.8 copy-start.10
  214.9 7.5 collective-permute-start.26
  217.4 4.7 collective-permute-start.27
  224.8 7.2 copy-start.35
  224.8 7.2 copy-start.37
  225.0 8.0 collective-permute-start.28
  230.1 7.0 collective-permute-start.29
  243.1 11.6 collective-permute-start.30
  246.9 5.4 collective-permute-start.31
  257.1 3.4 copy-start.19
  260.8 4.5 copy-start.41
  265.2 327.3 %all-reduce.12.cloned.1.call-start = ((), (), s32[]{:S(2)}) async-start(), calls=%async_computation | async-start | bytes 131072 | tf_op jit(solution)/shard_map/psum | solution.py:152
  (12 other events, 17.0 us)
Sparse Core Ops, SparseCore 0:
  265.3 79.1 all-reduce.13
  351.5 240.9 all-reduce.11
where the time goes:
time: 1210 us; the launch traced here: 1190 us
  matrix products  475 us (39%)
  waiting for transfers between devices  362 us (30%)
  loops' own time  98.3 us (8%)
  starting transfers between devices  89 us (7%)
  local copies, waits for them, and re-layouts  85.4 us (7%)
  other arithmetic  68.3 us (6%)
  between operations  15.9 us (1%)
    psum x1, waiting for transfers between devices, shards(): gram_whole = lax.psum(gram_local, ('gx', 'gy'))  245 us
    dot_general x128, matrix products, column_step(): column = jnp.dot(gram, picker, precision=lax.Precision.HIGHEST)  124 us
    dot_general x128, matrix products, column_step(): column = column - jnp.dot(lower, row_of, precision=lax.Precision.HIGHEST)  108 us
    dot_general x128, matrix products, row_step(): jnp.dot(row_of, inverse, precision=lax.Precision.HIGHEST)  107 us
    dot_general x128, matrix products, row_step(): row_of = jnp.dot(picker, lower, precision=lax.Precision.HIGHEST)  105 us
    another operation x1, loops' own time, lower_factor(): return lax.fori_loop(0, order, column_step, jnp.zeros_like(gram))  94 us
    unnamed x3, waiting for transfers between devices  78.1 us
    ppermute x16, starting transfers between devices, extended(): lax.ppermute(lax.slice_in_dim(block, block.shape[dim] - width, None, axis...  62.5 us
  transfers between devices with their start and end apart: 34, of which 17 were waited for; matrix products, arithmetic and copies ran while one was open for 5% of the time, Pallas kernels for 0%

commit v1 on v0

--- a/solution.py
+++ b/solution.py
@@ -149,7 +149,7 @@
         precision=lax.Precision.HIGHEST,
         preferred_element_type=jnp.float32,
     )
-    gram_whole = lax.psum(gram_local, ("gx", "gy"))
+    gram_whole = lax.psum(lax.psum(gram_local, "gy"), "gx")
     orthonormal, factor = orthogonalize(tall_block, gram_whole)
     basis = (math.sqrt(rows_total) * orthonormal).reshape(sketch.shape)
     return (current, basis, factor)

time: 1210 us -> 1140 us (0.942)
  waiting for transfers between devices: 362 us -> 299 us
    psum x1 -> x2, waiting for transfers between devices: 245 us -> 182 us  [shards(): gram_whole = lax.psum(lax.psum(gram_local, 'gy'), 'gx')]
    unnamed x3 -> x4, waiting for transfers between devices: 78.1 us -> 78.1 us
  transfers between devices with their start and end apart: 34 -> 35, of which waited for: 17 -> 18; matrix products, arithmetic and copies ran while one was open for 5% -> 5% of each run, Pallas kernels for 0% -> 0%
where the time goes in v1:
time: 1140 us; the launch traced here: 1130 us
  matrix products  478 us (42%)
  waiting for transfers between devices  299 us (26%)
  loops' own time  97 us (9%)
  starting transfers between devices  89 us (8%)
  local copies, waits for them, and re-layouts  85.4 us (7%)
  other arithmetic  68.3 us (6%)
  between operations  15.6 us (1%)
    psum x2, waiting for transfers between devices, shards(): gram_whole = lax.psum(lax.psum(gram_local, 'gy'), 'gx')  182 us
    dot_general x128, matrix products, column_step(): column = jnp.dot(gram, picker, precision=lax.Precision.HIGHEST)  124 us
    dot_general x128, matrix products, column_step(): column = column - jnp.dot(lower, row_of, precision=lax.Precision.HIGHEST)  111 us
    dot_general x128, matrix products, row_step(): jnp.dot(row_of, inverse, precision=lax.Precision.HIGHEST)  107 us
    dot_general x128, matrix products, row_step(): row_of = jnp.dot(picker, lower, precision=lax.Precision.HIGHEST)  105 us
    another operation x1, loops' own time, lower_factor(): return lax.fori_loop(0, order, column_step, jnp.zeros_like(gram))  92.8 us
    unnamed x4, waiting for transfers between devices  78.1 us
    ppermute x16, starting transfers between devices, extended(): lax.ppermute(lax.slice_in_dim(block, block.shape[dim] - width, None, axis...  62.5 us
  transfers between devices with their start and end apart: 35, of which 18 were waited for; matrix products, arithmetic and copies ran while one was open for 5% of the time, Pallas kernels for 0%

profile of v1, /device:TPU:1, one launch (start us, length us, event | category | flops | bytes accessed | tf_op | source)
XLA Modules:
  0.0 1132.7 jit_solution(15672865155523736554)
XLA Ops:
  8.8 4.6 collective-permute-start
  13.4 2.0 collective-permute-start.1
  18.1 4.4 collective-permute-done.1
  26.6 4.9 collective-permute-start.2
  35.1 3.8 fusion.119
  42.7 1.8 fusion.162
  44.9 2.1 collective-permute-start.4
  47.0 2.2 collective-permute-start.5
  49.6 4.4 collective-permute-done.5
  56.2 2.4 copy.319
  59.1 3.6 collective-permute-start.6
  64.0 2.7 fusion.51
  69.5 2.4 copy.318
  71.9 3.0 fusion.94
  76.9 3.5 collective-permute-start.8
  80.4 1.9 collective-permute-start.9
  82.4 4.0 collective-permute-done.9
  89.0 3.7 collective-permute-start.10
  95.2 2.7 collective-permute-done.11
  99.3 2.1 fusion.155
  101.8 3.0 collective-permute-start.12
  104.8 1.9 collective-permute-start.13
  107.4 4.4 collective-permute-done.13
  111.8 1.8 fusion.291
  117.2 5.1 collective-permute-start.14
  125.4 2.5 collective-permute-done.15
  128.0 2.4 copy.332
  131.9 3.4 fusion.88
  136.6 2.9 collective-permute-start.16
  139.5 1.9 collective-permute-start.17
  141.4 6.0 slice.1072
  150.9 3.6 collective-permute-start.18
  157.0 2.4 collective-permute-done.19
  160.8 2.1 fusion.148
  163.3 5.1 collective-permute-start.20
  168.4 1.9 collective-permute-start.21
  171.9 6.0 slice.1074
  181.5 2.5 copy.342
  185.3 3.9 collective-permute-start.22
  190.5 2.7 fusion.41
  196.3 2.4 copy.341
  198.7 3.0 fusion.82
  202.2 5.1 collective-permute-start.24
  207.3 1.9 collective-permute-start.25
  210.9 2.5 slice.1076
  214.9 2.5 collective-permute-start.26
  220.1 2.0 collective-permute-done.27
  222.8 1.8 fusion.141
  225.0 5.1 collective-permute-start.28
  230.1 1.9 collective-permute-start.29
  233.0 4.0 collective-permute-done.29
  237.2 1.8 fusion.289
  239.0 2.4 copy.353
  243.1 3.7 collective-permute-start.30
  249.5 2.8 collective-permute-done.31
  252.3 2.4 copy.354
  254.7 2.4 copy.352
  257.1 3.4 fusion.76
  261.0 2.5 slice.1078
  266.5 78.0 %all-reduce.17.cloned.1.call-done = f32[4,48,128]{2,0,1:T(4,128)} async-done(((f32[4,48,128]{2,0,1:T(4,128)}), f32[4,48,128]{2,0,1:T(4,128)}) %all-reduce.17.cloned.1.call-update) | async-done | bytes 98320
  346.3 70.7 %all-reduce.13.cloned.1.call-done = f32[128,128]{1,0:T(8,128)} async-done(((f32[128,128]{1,0:T(8,128)}), f32[128,128]{1,0:T(8,128)}) %all-reduce.13.cloned.1.call-update) | async-done | bytes 65552 | tf_op jit(solution)/shard_map/psum | solution.py:152
  418.0 111.6 %all-reduce.15.cloned.1.call-done = f32[128,128]{1,0:T(8,128)} async-done(((f32[128,128]{1,0:T(8,128)}), f32[128,128]{1,0:T(8,128)}) %all-reduce.15.cloned.1.call-update) | async-done | bytes 65552 | tf_op jit(solution)/shard_map/psum | solution.py:152
  529.6 365.0 %while.30 = (s32[]{:T(128)}, f32[128,128]{1,0:T(8,128)S(1)}, f32[128,128]{1,0:T(8,128)}, s32[]{:T(128)}, s32[]{:T(128)}) while((s32[]{:T(128)}, f32[128,128]{1,0:T(8,128)S(1)}, f32[128,128]{1,0:T(8,128)}, s32[]{:T(128)}, s32[]{:T(128)}) %tuple.125), condition=%wide.region_8.9_spmd.clone.clone, body=%wide.region_6.8_spmd.clone.clone.sunk | while | flops 673410 | bytes 332917 | solution.py:96
  895.3 230.0 %while.29 = (s32[]{:T(128)}, f32[128,128]{1,0:T(8,128)S(1)}, f32[128,128]{1,0:T(8,128)S(1)}, s32[]{:T(128)}, s32[]{:T(128)}) while((s32[]{:T(128)}, f32[128,128]{1,0:T(8,128)S(1)}, f32[128,128]{1,0:T(8,128)S(1)}, s32[]{:T(128)}, s32[]{:T(128)}) %tuple.128), condition=%wide.region_11.12_spmd.clone, body=%wide.region_9.11_spmd.clone.sunk | while | flops 460034 | bytes 265316 | solution.py:110
  (1512 shorter events, 577.9 us)
Async XLA Ops:
  7.2 337.4 %all-reduce.17.cloned.1.call-start = ((), (), s32[]{:S(2)}) async-start(), calls=%async_computation.2 | async-start | bytes 196608
  8.7 6.7 copy-start.38
  8.7 6.7 copy-start.39
  8.7 6.8 copy-start.3
  8.8 7.5 copy-start.2
  8.8 9.3 collective-permute-start
  13.4 9.1 collective-permute-start.1
  15.5 29.0 %copy-start.4 = (f32[1,32,8,128]{3,2,1,0:T(8,128)}, f32[1,32,8,128]{3,2,1,0:T(8,128)S(1)}, u32[]{:S(2)}) copy-start(f32[1,32,8,128]{3,2,1,0:T(8,128)S(1)} %get-tuple-element.324) | copy-start | bytes 393220
  18.1 4.7 copy-start.23
  25.3 16.2 %collective-permute-start.3 = (f32[3,32,12,2]{1,3,2,0:T(2,128)}, f32[3,32,12,2]{1,3,2,0:T(2,128)}, u32[]{:S(2)}, u32[]{:S(2)}) collective-permute-start(f32[3,32,12,2]{1,3,2,0:T(2,128)} %get-tuple-element.276), channel_id=1, source_target_pairs={{1,0},{2,1},{3,2},{4,3},{5,4},{6,5},{7,6},{9,8},{10,9},{11,10},{12... | collective-permute-start | bytes 27656 | tf_op jit(solution)/shard_map/ppermute | solution.py:19
  26.6 12.3 %copy-start.1 = (f32[3,32,12,128]{1,3,2,0:T(8,128)S(1)}, f32[3,32,12,128]{1,3,2,0:T(8,128)}, u32[]{:S(2)}) copy-start(f32[3,32,12,128]{1,3,2,0:T(8,128)} %copy-done) | copy-start | bytes 1769476
  26.6 13.8 %collective-permute-start.2 = (f32[3,32,12,2]{1,3,2,0:T(2,128)}, f32[3,32,12,2]{1,3,2,0:T(2,128)}, u32[]{:S(2)}, u32[]{:S(2)}) collective-permute-start(f32[3,32,12,2]{1,3,2,0:T(2,128)} %get-tuple-element.277), channel_id=1, source_target_pairs={{0,1},{1,2},{2,3},{3,4},{4,5},{5,6},{6,7},{8,9},{9,10},{10,11},{11... | collective-permute-start | bytes 27656 | tf_op jit(solution)/shard_map/ppermute | solution.py:16
  40.4 2.2 copy-start.9
  40.4 2.2 copy-start.14
  44.7 4.5 copy-start.40
  44.9 4.7 collective-permute-start.4
  47.0 7.0 collective-permute-start.5
  49.6 4.4 copy-start.17
  59.1 10.4 collective-permute-start.6
  62.7 5.4 collective-permute-start.7
  71.9 3.0 copy-start.11
  71.9 3.0 copy-start.20
  76.9 5.5 collective-permute-start.8
  80.4 5.9 collective-permute-start.9
  86.4 7.7 copy-start.30
  89.0 9.1 collective-permute-start.10
  92.8 5.1 collective-permute-start.11
  95.2 4.1 copy-start.31
  101.8 5.6 collective-permute-start.12
  104.8 7.0 collective-permute-start.13
  117.2 13.2 %collective-permute-start.14 = (f32[6,32,12,2]{1,3,2,0:T(2,128)S(1)}, f32[6,32,12,2]{1,3,2,0:T(2,128)S(1)}, u32[]{:S(2)}, u32[]{:S(2)}) collective-permute-start(f32[6,32,12,2]{1,3,2,0:T(2,128)S(1)} %copy.329), channel_id=1, source_target_pairs={{0,1},{1,2},{2,3},{3,4},{4,5},{5,6},{6,7},{8,9},{9,10},{10,11},{11... | collective-permute-start | bytes 55304 | tf_op jit(solution)/shard_map/ppermute | solution.py:16
  122.3 5.7 collective-permute-start.15
  131.9 3.5 copy-start.12
  131.9 3.5 copy-start.21
  136.6 11.5 %collective-permute-start.16 = (f32[3,32,2,128]{3,1,2,0:T(8,128)S(1)}, f32[3,32,2,128]{3,1,2,0:T(8,128)S(1)}, u32[]{:S(2)}, u32[]{:S(2)}) collective-permute-start(f32[3,32,2,128]{3,1,2,0:T(8,128)S(1)} %get-tuple-element.316), channel_id=1, source_target_pairs={{0,8},{8,16},{16,24},{24,32},{32,40},{40,48},{48,56},{56,64},{64,7... | collective-permute-start | bytes 294920 | tf_op jit(solution)/shard_map/ppermute | solution.py:16
  139.5 8.6 collective-permute-start.17
  150.9 8.8 collective-permute-start.18
  154.5 4.8 collective-permute-start.19
  163.1 7.2 copy-start.33
  163.3 15.3 %collective-permute-start.20 = (f32[6,32,2,128]{3,1,2,0:T(8,128)S(1)}, f32[6,32,2,128]{3,1,2,0:T(8,128)S(1)}, u32[]{:S(2)}, u32[]{:S(2)}) collective-permute-start(f32[6,32,2,128]{3,1,2,0:T(8,128)S(1)} %get-tuple-element.294), channel_id=1, source_target_pairs={{0,8},{8,16},{16,24},{24,32},{32,40},{40,48},{48,56},{56,64},{64,7... | collective-permute-start | bytes 589832 | tf_op jit(solution)/shard_map/ppermute | solution.py:16
  168.4 10.2 collective-permute-start.21
  185.3 11.0 collective-permute-start.22
  189.3 5.7 collective-permute-start.23
  198.7 3.0 copy-start.13
  198.7 3.0 copy-start.22
  202.0 7.2 copy-start.34
  202.0 7.2 copy-start.36
  202.2 11.8 %collective-permute-start.24 = (f32[3,32,2,128]{3,1,2,0:T(8,128)S(1)}, f32[3,32,2,128]{3,1,2,0:T(8,128)S(1)}, u32[]{:S(2)}, u32[]{:S(2)}) collective-permute-start(f32[3,32,2,128]{3,1,2,0:T(8,128)S(1)} %get-tuple-element.312), channel_id=1, source_target_pairs={{0,8},{8,16},{16,24},{24,32},{32,40},{40,48},{48,56},{56,64},{64,7... | collective-permute-start | bytes 294920 | tf_op jit(solution)/shard_map/ppermute | solution.py:16
  207.3 6.7 collective-permute-start.25
  214.0 4.9 copy-start.29
  214.9 7.8 copy-start.8
  214.9 7.8 copy-start.10
  214.9 7.5 collective-permute-start.26
  217.4 4.7 collective-permute-start.27
  224.8 7.2 copy-start.35
  224.8 7.2 copy-start.37
  225.0 8.0 collective-permute-start.28
  230.1 7.0 collective-permute-start.29
  243.1 11.6 %collective-permute-start.30 = (f32[6,32,12,2]{1,3,2,0:T(2,128)S(1)}, f32[6,32,12,2]{1,3,2,0:T(2,128)}, u32[]{:S(2)}, u32[]{:S(2)}) collective-permute-start(f32[6,32,12,2]{1,3,2,0:T(2,128)S(1)} %copy.351), channel_id=1, source_target_pairs={{0,1},{1,2},{2,3},{3,4},{4,5},{5,6},{6,7},{8,9},{9,10},{10,11},{11... | collective-permute-start | bytes 55304 | tf_op jit(solution)/shard_map/ppermute | solution.py:16
  246.9 5.4 collective-permute-start.31
  257.1 3.4 copy-start.19
  260.8 4.5 copy-start.41
  265.2 151.7 %all-reduce.13.cloned.1.call-start = ((), (), s32[]{:S(2)}) async-start(), calls=%async_computation | async-start | bytes 131072 | tf_op jit(solution)/shard_map/psum | solution.py:152
  346.2 183.4 %all-reduce.15.cloned.1.call-start = ((), (), s32[]{:S(2)}) async-start(), calls=%async_computation.1 | async-start | bytes 131072 | tf_op jit(solution)/shard_map/psum | solution.py:152
  (13 other events, 19.2 us)
Sparse Core Ops, SparseCore 0:
  265.3 79.1 all-reduce.16
  347.5 69.3 all-reduce.12
  420.2 109.3 all-reduce.14
